TPU v7x, 512 devices: a whole 4x4x16 slice. The times are simulated.
512 devices in a mesh: seq: 64 (over z, x), head: 8 (over y, core).
Axes of the slice: x: 4, y: 4, z: 16, core: 2. Of those that a mesh axis runs over, the one named last changes fastest.
Arguments:
- hidden: bfloat16 [32768, 4096], P('seq'), may hold values from -6 to 6
- steer: bfloat16 [4096], replicated, may hold values from -4 to 4
- w_x: bfloat16 [4096, 4096], P('seq', 'head'), may hold values from -0.09375 to 0.09375
- w_z: bfloat16 [4096, 4096], P('seq', 'head'), may hold values from -0.09375 to 0.09375
- w_shared: bfloat16 [4096, 320], P(('seq', 'head')), may hold values from -0.09375 to 0.09375
- conv_x: float32 [4, 4096], P(None, 'head'), may hold values from -3 to 3
- conv_shared: float32 [4, 256], replicated, may hold values from -3 to 3
- dt_bias: float32 [64], P('head'), may hold values from -7 to 0
- decay_rate: float32 [64], P('head'), may hold values from 0.01 to 16
- skip: float32 [64], P('head'), may hold values from 0.5 to 1.5
- norm_gain: float32 [4096], P('head'), may hold values from 0.5 to 1.5
Outputs:
- mixed: bfloat16 [32768, 4096], P('seq', 'head')
All inputs are finite; a program needn't handle non-finite values.
Results may differ from a plain program's by a relative error of at most 0.0095.
Values may be sent and summed in bfloat16 or wider, within the bound.
No kernel may reach another device: no remote copies, remote signals or barrier semaphores. Data moves between devices by JAX's collectives and lax.ppermute only.
A program may use at most 128 MiB of HBM per device.

v0:
```python
import jax
import jax.numpy as jnp
from jax import lax
from jax.sharding import PartitionSpec as P

STATE = 128
CONV = 4
SPAN = 128
highest = lax.Precision.HIGHEST


def shifted(block, axis, distance):
    devices = range(lax.axis_size(axis))
    route = [(i - distance, i) for i in devices if i - distance in devices]
    return lax.ppermute(block, axis, route)


def carried_in(shard, axis, combine, identity):
    count, position = (lax.axis_size(axis), lax.axis_index(axis))
    everything = jax.tree.map(
        lambda part, kind: lax.all_gather(part.astype(kind), axis),
        shard,
        (jnp.bfloat16, jnp.bfloat16),
    )
    start = jax.tree.map(
        lambda part, zero: jnp.broadcast_to(jnp.asarray(zero, part.dtype), part.shape),
        shard,
        identity,
    )

    def step(k, before):
        reached = k < position
        new = combine(
            before, jax.tree.map(lambda part, own: part[k].astype(own.dtype), everything, shard)
        )
        return jax.tree.map(lambda a, b: jnp.where(reached, a, b), new, before)

    return lax.fori_loop(0, count, step, start)


def conv_valid(extended, weights):
    taps = weights.shape[0]
    count = extended.shape[0] - taps + 1
    values = extended.astype(jnp.float32)
    total = jnp.zeros((count, extended.shape[1]), jnp.float32)
    for k in range(taps):
        total = total + values[k : k + count] * weights[k]
    return total


def span_pass(inputs, steps, logs, in_map, out_map, start):
    blocks = inputs.shape[0] // SPAN
    heads = inputs.shape[1]
    width = inputs.shape[2]
    index = jnp.arange(SPAN)
    lower = index[:, None] >= index[None, :]

    def advance(state, block):
        xblock, dblock, lblock, bblock, cblock = block
        cums = jnp.cumsum(lblock, axis=0)
        gram = jnp.dot(cblock, bblock.T, precision=highest)
        diff = cums[:, None, :] - cums[None, :, :]
        decay = jnp.exp(jnp.where(lower[:, :, None], diff, -1e30))
        weights = gram[:, :, None] * decay * dblock[None, :, :]
        within = jnp.einsum("ijh,jhp->ihp", weights, xblock, precision=highest)
        carried = (
            jnp.einsum("in,hpn->ihp", cblock, state, precision=highest) * jnp.exp(cums)[:, :, None]
        )
        tail = jnp.exp(cums[-1][None, :] - cums) * dblock
        fresh = jnp.einsum("jh,jhp,jn->hpn", tail, xblock, bblock, precision=highest)
        state = jnp.exp(cums[-1])[:, None, None] * state + fresh
        return (state, within + carried)

    final, outs = lax.scan(
        advance,
        start,
        (
            inputs.reshape(blocks, SPAN, heads, width),
            steps.reshape(blocks, SPAN, heads),
            logs.reshape(blocks, SPAN, heads),
            in_map.reshape(blocks, SPAN, in_map.shape[1]),
            out_map.reshape(blocks, SPAN, out_map.shape[1]),
        ),
    )
    return (outs.reshape(-1, heads, width), final)


def combine_states(earlier, later):
    return (earlier[0] + later[0], jnp.exp(later[0])[:, None, None] * earlier[1] + later[1])


def on_device(
    hidden, steer, w_x, w_z, w_shared, conv_x, conv_shared, dt_bias, decay_rate, skip, norm_gain
):
    rows = hidden.shape[0]
    edge = CONV - 1
    head_count = dt_bias.shape[0]
    width = w_x.shape[1]
    head_index = lax.axis_index("head")
    steered = (hidden.astype(jnp.float32) + steer.astype(jnp.float32)).astype(jnp.bfloat16)
    columns = steered
    x_sum = jnp.dot(
        columns, lax.all_gather(w_x, "seq", axis=0, tiled=True), preferred_element_type=jnp.float32
    )
    z_sum = jnp.dot(
        columns, lax.all_gather(w_z, "seq", axis=0, tiled=True), preferred_element_type=jnp.float32
    )
    columns = steered
    shared = jnp.dot(
        columns,
        lax.all_gather(w_shared, ("seq", "head"), axis=0, tiled=True),
        preferred_element_type=jnp.float32,
    )
    x_raw = x_sum.astype(jnp.bfloat16)
    z_raw = z_sum.astype(jnp.bfloat16)
    b_raw = shared[:, : 2 * STATE].astype(jnp.bfloat16)
    dt_raw = shared[:, 2 * STATE :]
    x_prev, b_prev = shifted((x_raw[rows - edge :], b_raw[rows - edge :]), "seq", 1)
    x_ext = jnp.concatenate([x_prev, x_raw], axis=0)
    b_ext = jnp.concatenate([b_prev, b_raw], axis=0)
    x_conv = jax.nn.silu(conv_valid(x_ext, conv_x)).astype(jnp.bfloat16)
    b_conv = jax.nn.silu(conv_valid(b_ext, conv_shared)).astype(jnp.bfloat16)
    in_map = b_conv[:, :STATE].astype(jnp.float32)
    out_map = b_conv[:, STATE:].astype(jnp.float32)
    dt_mine = lax.dynamic_slice_in_dim(dt_raw, head_index * head_count, head_count, 1)
    steps = jax.nn.softplus(dt_mine + dt_bias)
    logs = -steps * decay_rate
    inputs = x_conv.astype(jnp.float32).reshape(rows, head_count, width // head_count)
    start = jnp.zeros((head_count, width // head_count, STATE), jnp.float32)
    heads_out, final = span_pass(inputs, steps, logs, in_map, out_map, start)
    total_log = jnp.sum(logs, axis=0)
    identity = (jnp.zeros_like(total_log), jnp.zeros_like(final))
    log_in, state_in = carried_in((total_log, final), "seq", combine_states, identity)
    running = jnp.cumsum(logs, axis=0)
    incoming = (
        jnp.einsum("tn,hpn->thp", out_map, state_in, precision=highest)
        * jnp.exp(running)[:, :, None]
    )
    heads_out = heads_out + incoming + skip[None, :, None] * inputs
    gated = heads_out.reshape(rows, width) * jax.nn.silu(z_raw.astype(jnp.float32))
    squares = lax.psum(jnp.sum(gated * gated, axis=1), "head")
    total_width = width * lax.axis_size("head")
    scale = lax.rsqrt(squares / total_width + 1e-05)
    return (gated * scale[:, None] * norm_gain).astype(jnp.bfloat16)


def solution(mesh):
    placed = (
        P("seq", None),
        P(),
        P("seq", "head"),
        P("seq", "head"),
        P(("seq", "head"), None),
        P(None, "head"),
        P(),
        P("head"),
        P("head"),
        P("head"),
        P("head"),
    )
    return jax.shard_map(
        on_device, mesh=mesh, in_specs=placed, out_specs=P("seq", "head"), check_vma=False
    )
```

profile of v0, /device:TPU:1, one launch (start us, length us, event | category | flops | bytes accessed | tf_op | source)
XLA Modules:
  0.0 753.1 jit_solution(3623105152973031940)
XLA Ops:
  10.5 203.2 %all-gather.7.cloned.1.call-done = bf16[4096,320]{1,0:T(8,128)(2,1)} async-done(((bf16[8,320]{1,0:T(8,128)(2,1)}), bf16[4096,320]{1,0:T(8,128)(2,1)}) %all-gather.7.cloned.1.call-update) | async-done | bytes 2621456 | tf_op jit(solution)/shard_map/all_gather | solution.py:111
  213.7 4.8 fusion.65
  218.6 3.2 collective-permute-start.1
  223.9 125.1 %all-gather.9.cloned.1.call-done = bf16[4096,512]{1,0:T(8,128)(2,1)} async-done(((bf16[64,512]{1,0:T(8,128)(2,1)}), bf16[4096,512]{1,0:T(8,128)(2,1)}) %all-gather.9.cloned.1.call-update) | async-done | bytes 4194320 | tf_op jit(solution)/shard_map/all_gather | solution.py:103
  349.0 5.8 fusion.43
  354.8 1.7 collective-permute-start
  359.5 1.6 copy.51
  361.1 56.6 %while.27 = (s32[]{:T(128)}, f32[8,64,128]{2,1,0:T(8,128)S(1)}, f32[4,128,8,64]{1,0,3,2:T(4,128)}, f32[4,128,8]{1,2,0:T(8,128)S(1)}, f32[4,128,8]{1,2,0:T(8,128)...) while((s32[]{:T(128)}, f32[8,64,128]{2,1,0:T(8,128)S(1)}, ...), condition=%wide.region_2.3_spmd.clone, body=%wide.region_0.2_spmd.clone.sunk | while | flops 328287232 | bytes 3153220 | solution.py:74
  362.6 2.1 convolution_bitcast_fusion.2
  366.2 7.5 dynamic_update_slice.6
  373.8 1.5 convolution_add_fusion.2
  376.8 2.1 convolution_bitcast_fusion.2
  379.1 1.2 fusion.92
  380.3 7.5 dynamic_update_slice.6
  387.9 1.5 convolution_add_fusion.2
  390.9 2.1 convolution_bitcast_fusion.2
  393.2 1.2 fusion.92
  394.5 7.5 dynamic_update_slice.6
  402.1 1.5 convolution_add_fusion.2
  405.1 2.1 convolution_bitcast_fusion.2
  407.4 1.2 fusion.92
  408.7 7.5 dynamic_update_slice.6
  416.2 1.5 convolution_add_fusion.2
  419.0 1.3 dynamic-slice
  421.2 114.6 %all-reduce = bf16[512]{0:T(512)(128)(2,1)S(1)} all-reduce(bf16[512]{0:T(512)(128)(2,1)S(1)} %dynamic-update-slice), channel_id=2, replica_groups=mesh['seq'=64,'head'=8] {'seq'}, use_global_device_ids=true, to_apply=%add | all-reduce | flops 512 | bytes 2048
  537.7 1.7 reshape.83
  539.4 36.1 %all-gather.13.cloned.1.call-done = bf16[512,64,128]{2,1,0:T(8,128)(2,1)} async-done(((bf16[8,64,128]{2,1,0:T(8,128)(2,1)}), bf16[512,64,128]{2,1,0:T(8,128)(2,1)}) %all-gather.13.cloned.1.call-update) | async-done | bytes 8388624 | tf_op jit(solution)/shard_map/all_gather | solution.py:21
  575.4 67.5 %while.28 = (s32[]{:T(128)}, f32[8,64,128]{2,1,0:T(8,128)S(1)}, s32[]{:T(128)}, bf16[64,8]{1,0:T(8,128)(2,1)S(1)}, bf16[64,8,64,128]{3,2,1,0:T(8,128)(2,1)}, /*index=5*/s32[]{:T(128)}, s32[]{:T(128)}) while((s32[]{:T(128)}, f32[8,64,128]{2,1,0:T(8,128)S(1)}, s32[]{:T(128)}, bf16[64,8]{1,0:T(8,128)(2,1)S(1)}, ...), condition=%wide.region_5.6_spmd.clone, body=%wide.region_4.5_spmd.clone.sunk | while | flops 327692 | bytes 655545 | solution.py:38
  642.9 1.5 fusion.42
  644.9 73.1 %all-gather.11.cloned.1.call-done = bf16[4096,512]{1,0:T(8,128)(2,1)} async-done(((bf16[64,512]{1,0:T(8,128)(2,1)}), bf16[4096,512]{1,0:T(8,128)(2,1)}) %all-gather.11.cloned.1.call-update) | async-done | bytes 4194320 | tf_op jit(solution)/shard_map/all_gather | solution.py:106
  718.0 6.1 multiply_reduce_fusion
  724.0 21.6 %psum.7 = f32[512]{0:T(512)S(1)} all-reduce(f32[512]{0:T(512)S(1)} %get-tuple-element.267), channel_id=1, replica_groups=mesh['seq'=64,'head'=8] {'head'}, use_global_device_ids=true, to_apply=%region_9.10 | all-reduce | flops 512 | bytes 4096 | tf_op jit(solution)/shard_map/psum | solution.py:141
  (229 shorter events, 87.4 us)
Async XLA Ops:
  6.5 207.2 %all-gather.7.cloned.1.call-start = ((), (), s32[]{:S(2)}) async-start(), calls=%async_computation | async-start | bytes 3151872 | tf_op jit(solution)/shard_map/all_gather | solution.py:111
  7.3 341.7 %all-gather.9.cloned.1.call-start = ((), (), s32[]{:S(2)}) async-start(), calls=%async_computation.1 | async-start | bytes 4259840 | tf_op jit(solution)/shard_map/all_gather | solution.py:103
  8.0 567.4 %all-gather.13.cloned.1.call-start = ((), (), s32[]{:S(2)}) async-start(), calls=%async_computation.3 | async-start | bytes 8519680 | tf_op jit(solution)/shard_map/all_gather | solution.py:21
  10.5 211.3 %copy-start.2 = (f32[8]{0:T(128)S(1)}, f32[8]{0:T(128)}, u32[]{:S(2)}) copy-start(f32[8]{0:T(128)} %param.23) | copy-start | bytes 100
  10.5 211.3 %copy-start.3 = (f32[8]{0:T(128)S(1)}, f32[8]{0:T(128)}, u32[]{:S(2)}) copy-start(f32[8]{0:T(128)} %param.22) | copy-start | bytes 100
  218.6 4.5 collective-permute-start.1
  223.9 132.6 %copy-start = (bf16[512,256]{0,1:T(8,128)(2,1)}, bf16[512,256]{0,1:T(8,128)(2,1)S(1)}, u32[]{:S(2)}) copy-start(bf16[512,256]{0,1:T(8,128)(2,1)S(1)} %multiply_convert_fusion.2) | copy-start | bytes 786436
  354.8 3.5 collective-permute-start
  417.7 225.2 %copy-start.4 = (f32[8]{0:T(128)S(1)}, f32[8]{0:T(128)}, u32[]{:S(2)}) copy-start(f32[8]{0:T(128)} %param.24) | copy-start | bytes 100
  418.4 299.5 %all-gather.11.cloned.1.call-start = ((), (), s32[]{:S(2)}) async-start(), calls=%async_computation.2 | async-start | bytes 4259840 | tf_op jit(solution)/shard_map/all_gather | solution.py:106
  644.8 100.8 %copy-start.1 = (f32[512]{0:T(512)S(1)}, f32[512]{0:T(512)}, u32[]{:S(2)}) copy-start(f32[512]{0:T(512)} %param.25) | copy-start | bytes 6148
Sparse Core Ops, SparseCore 0:
  11.7 201.9 all-gather.6
  216.7 132.3 all-gather.8
  418.5 156.8 all-gather.12
  578.2 139.6 all-gather.10
where the time goes:
time: 756 us; the launch traced here: 753 us
  waiting for transfers between devices  440 us (58%)
  blocking collectives  136 us (18%)
  other arithmetic  71.9 us (10%)
  matrix products  42.1 us (6%)
  local copies, waits for them, and re-layouts  41.2 us (5%)
  between operations  14 us (2%)
    all_gather x1, waiting for transfers between devices, on_device(): lax.all_gather(w_shared, ('seq', 'head'), axis=0, tiled=True)  203 us
    all_gather x1, waiting for transfers between devices, on_device(): lax.all_gather(w_x, 'seq', axis=0, tiled=True)  125 us
    unnamed x1, blocking collectives  115 us
    all_gather x1, waiting for transfers between devices, on_device(): lax.all_gather(w_z, 'seq', axis=0, tiled=True)  73.1 us
    select_n x64, other arithmetic, step(): return jax.tree.map(lambda a, b: jnp.where(reached, a, b), new, before)  64.8 us
    all_gather x1, waiting for transfers between devices, carried_in(): lax.all_gather(part.astype(kind), axis)  36.1 us
    dynamic_update_slice x4, local copies, waits for them, and re-layouts, span_pass(): lax.scan(advance, start, (inputs.reshape(blocks, SPAN, heads, width), ste...  30.1 us
    psum x1, blocking collectives, on_device(): squares = lax.psum(jnp.sum(gated * gated, axis=1), 'head')  21.6 us
  transfers between devices with their start and end apart: 6, of which 5 were waited for; matrix products, arithmetic and copies ran while one was open for 11% of the time, Pallas kernels for 0%

commit v1 on v0

--- a/solution.py
+++ b/solution.py
@@ -108,7 +108,12 @@
     columns = steered
     shared = jnp.dot(
         columns,
-        lax.all_gather(w_shared, ("seq", "head"), axis=0, tiled=True),
+        jnp.concatenate(
+            lax.all_to_all(
+                jnp.stack([w_shared] * lax.axis_size(("seq", "head"))), ("seq", "head"), 0, 0
+            ),
+            axis=0,
+        ),
         preferred_element_type=jnp.float32,
     )
     x_raw = x_sum.astype(jnp.bfloat16)

time: 756 us -> 618 us (0.82)
  waiting for transfers between devices: 440 us -> 285 us
  starting transfers between devices: 5.01 us -> 33.2 us
  matrix products: 42.1 us -> 27.7 us
    all_gather x1 -> x0, waiting for transfers between devices: 203 us -> none  [on_device(): lax.all_gather(w_shared, ('seq', 'head'), axis=0, tiled=True)]
    all_gather x1, waiting for transfers between devices: 125 us -> 175 us  [on_device(): lax.all_gather(w_x, 'seq', axis=0, tiled=True)]
    all_to_all x0 -> x1, starting transfers between devices: none -> 26.1 us  [on_device(): lax.all_to_all(jnp.stack([w_shared] * lax.axis_size(('seq', 'head'))), ('...]
  transfers between devices with their start and end apart: 6 -> 6, of which waited for: 5 -> 5; matrix products, arithmetic and copies ran while one was open for 11% -> 13% of each run, Pallas kernels for 0% -> 0%
where the time goes in v1:
time: 618 us; the launch traced here: 616 us
  waiting for transfers between devices  285 us (46%)
  blocking collectives  137 us (22%)
  other arithmetic  72.9 us (12%)
  local copies, waits for them, and re-layouts  44.3 us (7%)
  starting transfers between devices  33.2 us (5%)
  matrix products  27.7 us (4%)
  between operations  14.2 us (2%)
    all_gather x1, waiting for transfers between devices, on_device(): lax.all_gather(w_x, 'seq', axis=0, tiled=True)  175 us
    unnamed x1, blocking collectives  115 us
    all_gather x1, waiting for transfers between devices, on_device(): lax.all_gather(w_z, 'seq', axis=0, tiled=True)  73.6 us
    select_n x64, other arithmetic, step(): return jax.tree.map(lambda a, b: jnp.where(reached, a, b), new, before)  64.8 us
    all_gather x1, waiting for transfers between devices, carried_in(): lax.all_gather(part.astype(kind), axis)  33.8 us
    dynamic_update_slice x4, local copies, waits for them, and re-layouts, span_pass(): lax.scan(advance, start, (inputs.reshape(blocks, SPAN, heads, width), ste...  30.1 us
    all_to_all x1, starting transfers between devices, on_device(): lax.all_to_all(jnp.stack([w_shared] * lax.axis_size(('seq', 'head'))), ('...  26.1 us
    psum x1, blocking collectives, on_device(): squares = lax.psum(jnp.sum(gated * gated, axis=1), 'head')  21.6 us
  transfers between devices with their start and end apart: 6, of which 5 were waited for; matrix products, arithmetic and copies ran while one was open for 13% of the time, Pallas kernels for 0%

profile of v1, /device:TPU:1, one launch (start us, length us, event | category | flops | bytes accessed | tf_op | source)
XLA Modules:
  0.0 615.8 jit_solution(12993572222781899122)
XLA Ops:
  6.5 2.7 stack.2
  9.2 26.1 %all-to-all-start = ((bf16[512,8,320]{2,1,0:T(8,128)(2,1)}), bf16[512,8,320]{2,1,0:T(8,128)(2,1)}, u32[]{:S(2)}, u32[]{:S(2)}) async-start(bf16[512,8,320]{2,1,0:T(8,128)(2,1)} %stack.2), calls=%async_computation | async-start | bytes 6291456 | tf_op jit(solution)/shard_map/all_to_all | solution.py:112
  36.2 175.1 %all-gather.6.cloned.1.call-done = bf16[4096,512]{1,0:T(8,128)(2,1)} async-done(((bf16[64,512]{1,0:T(8,128)(2,1)}), bf16[4096,512]{1,0:T(8,128)(2,1)}) %all-gather.6.cloned.1.call-update) | async-done | bytes 4194320 | tf_op jit(solution)/shard_map/all_gather | solution.py:103
  211.3 5.8 fusion.44
  217.1 3.1 collective-permute-start
  222.1 1.6 copy.51
  223.8 4.8 fusion.66
  228.6 3.9 collective-permute-start.1
  235.5 44.9 %while.27 = (s32[]{:T(128)}, f32[8,64,128]{2,1,0:T(8,128)S(1)}, f32[4,128,8,64]{1,0,3,2:T(4,128)}, f32[4,128,8]{1,2,0:T(8,128)}, f32[4,128,8]{1,2,0:T(8,128)}, /...) while((s32[]{:T(128)}, f32[8,64,128]{2,1,0:T(8,128)S(1)}, ...), condition=%wide.region_2.3_spmd.clone, body=%wide.region_0.2_spmd.clone.sunk | while | flops 328287232 | bytes 3152684 | solution.py:74
  236.9 1.2 convolution_bitcast_fusion.2
  238.7 7.5 %dynamic_update_slice.6 = f32[4,128,8,64]{1,0,3,2:T(4,128)} dynamic-update-slice(f32[4,128,8,64]{1,0,3,2:T(4,128)} %get-tuple-element.370, f32[1,128,8,64]{1,0,3,2:T(1,128)S(1)} %bitcast.102, s32[]{:T(128)} %get-tuple-element.368, s32[]{:T(128)} %constant.68.clone.1..sunk, s32[]{:T(128)} %constant.68.clone.1..sunk, s32[]{:T(128)} %constant.68.clone.1..sunk) | dynamic-update-slice | bytes 524292 | tf_op jit(solution)/shard_map/while/body/jit(dynamic_update_index_in_dim)/dynamic_update_slice | solution.py:74
  248.1 1.2 convolution_bitcast_fusion.2
  249.9 7.5 %dynamic_update_slice.6 = f32[4,128,8,64]{1,0,3,2:T(4,128)} dynamic-update-slice(f32[4,128,8,64]{1,0,3,2:T(4,128)} %get-tuple-element.370, f32[1,128,8,64]{1,0,3,2:T(1,128)S(1)} %bitcast.102, s32[]{:T(128)} %get-tuple-element.368, s32[]{:T(128)} %constant.68.clone.1..sunk, s32[]{:T(128)} %constant.68.clone.1..sunk, s32[]{:T(128)} %constant.68.clone.1..sunk) | dynamic-update-slice | bytes 524292 | tf_op jit(solution)/shard_map/while/body/jit(dynamic_update_index_in_dim)/dynamic_update_slice | solution.py:74
  259.3 1.2 convolution_bitcast_fusion.2
  261.1 7.5 %dynamic_update_slice.6 = f32[4,128,8,64]{1,0,3,2:T(4,128)} dynamic-update-slice(f32[4,128,8,64]{1,0,3,2:T(4,128)} %get-tuple-element.370, f32[1,128,8,64]{1,0,3,2:T(1,128)S(1)} %bitcast.102, s32[]{:T(128)} %get-tuple-element.368, s32[]{:T(128)} %constant.68.clone.1..sunk, s32[]{:T(128)} %constant.68.clone.1..sunk, s32[]{:T(128)} %constant.68.clone.1..sunk) | dynamic-update-slice | bytes 524292 | tf_op jit(solution)/shard_map/while/body/jit(dynamic_update_index_in_dim)/dynamic_update_slice | solution.py:74
  270.5 1.2 convolution_bitcast_fusion.2
  272.3 7.5 %dynamic_update_slice.6 = f32[4,128,8,64]{1,0,3,2:T(4,128)} dynamic-update-slice(f32[4,128,8,64]{1,0,3,2:T(4,128)} %get-tuple-element.370, f32[1,128,8,64]{1,0,3,2:T(1,128)S(1)} %bitcast.102, s32[]{:T(128)} %get-tuple-element.368, s32[]{:T(128)} %constant.68.clone.1..sunk, s32[]{:T(128)} %constant.68.clone.1..sunk, s32[]{:T(128)} %constant.68.clone.1..sunk) | dynamic-update-slice | bytes 524292 | tf_op jit(solution)/shard_map/while/body/jit(dynamic_update_index_in_dim)/dynamic_update_slice | solution.py:74
  281.9 1.3 dynamic-slice
  284.6 114.9 %all-reduce = bf16[512]{0:T(512)(128)(2,1)S(1)} all-reduce(bf16[512]{0:T(512)(128)(2,1)S(1)} %dynamic-update-slice), channel_id=2, replica_groups=mesh['seq'=64,'head'=8] {'seq'}, use_global_device_ids=true, to_apply=%add | all-reduce | flops 512 | bytes 2048
  399.6 2.2 reduce-window.6
  402.1 1.6 reshape.89
  403.7 33.8 %all-gather.10.cloned.1.call-done = bf16[512,64,128]{2,1,0:T(8,128)(2,1)} async-done(((bf16[8,64,128]{2,1,0:T(8,128)(2,1)}), bf16[512,64,128]{2,1,0:T(8,128)(2,1)}) %all-gather.10.cloned.1.call-update) | async-done | bytes 8388624 | tf_op jit(solution)/shard_map/all_gather | solution.py:21
  437.6 67.5 %while.28 = (s32[]{:T(128)}, f32[8,64,128]{2,1,0:T(8,128)S(1)}, s32[]{:T(128)}, bf16[64,8]{1,0:T(8,128)(2,1)S(1)}, bf16[64,8,64,128]{3,2,1,0:T(8,128)(2,1)}, /*index=5*/s32[]{:T(128)}, s32[]{:T(128)}) while((s32[]{:T(128)}, f32[8,64,128]{2,1,0:T(8,128)S(1)}, s32[]{:T(128)}, bf16[64,8]{1,0:T(8,128)(2,1)S(1)}, ...), condition=%wide.region_5.6_spmd.clone, body=%wide.region_4.5_spmd.clone.sunk | while | flops 327692 | bytes 655545 | solution.py:38
  464.0 1.0 fusion.93
  469.2 1.0 fusion.93
  476.6 1.0 fusion.93
  495.6 1.0 fusion.93
  497.7 1.0 fusion.93
  505.1 1.6 fusion.43
  507.0 73.6 %all-gather.8.cloned.1.call-done = bf16[4096,512]{1,0:T(8,128)(2,1)} async-done(((bf16[64,512]{1,0:T(8,128)(2,1)}), bf16[4096,512]{1,0:T(8,128)(2,1)}) %all-gather.8.cloned.1.call-update) | async-done | bytes 4194320 | tf_op jit(solution)/shard_map/all_gather | solution.py:106
  580.7 6.1 multiply_reduce_fusion
  586.7 21.6 %psum.7 = f32[512]{0:T(512)S(1)} all-reduce(f32[512]{0:T(512)S(1)} %get-tuple-element.267), channel_id=1, replica_groups=mesh['seq'=64,'head'=8] {'head'}, use_global_device_ids=true, to_apply=%region_9.10 | all-reduce | flops 512 | bytes 4096 | tf_op jit(solution)/shard_map/psum | solution.py:146
  (241 shorter events, 79.7 us)
Async XLA Ops:
  6.5 29.6 %copy-start.4 = (bf16[4096]{0:T(1024)(128)(2,1)S(1)}, bf16[4096]{0:T(1024)(128)(2,1)}, u32[]{:S(2)}) copy-start(bf16[4096]{0:T(1024)(128)(2,1)} %param.16) | copy-start | bytes 24580
  6.5 29.6 %copy-start.5 = (f32[4,512]{1,0:T(4,128)S(1)}, f32[4,512]{1,0:T(4,128)}, u32[]{:S(2)}) copy-start(f32[4,512]{1,0:T(4,128)} %param.20) | copy-start | bytes 24580
  9.2 214.5 %all-to-all-start = ((bf16[512,8,320]{2,1,0:T(8,128)(2,1)}), bf16[512,8,320]{2,1,0:T(8,128)(2,1)}, u32[]{:S(2)}, u32[]{:S(2)}) async-start(bf16[512,8,320]{2,1,0:T(8,128)(2,1)} %stack.2), calls=%async_computation | async-start | bytes 6291456 | tf_op jit(solution)/shard_map/all_to_all | solution.py:112
  35.3 175.9 %all-gather.6.cloned.1.call-start = ((), (), s32[]{:S(2)}) async-start(), calls=%async_computation.1 | async-start | bytes 4259840 | tf_op jit(solution)/shard_map/all_gather | solution.py:103
  36.1 401.5 %all-gather.10.cloned.1.call-start = ((), (), s32[]{:S(2)}) async-start(), calls=%async_computation.3 | async-start | bytes 8519680 | tf_op jit(solution)/shard_map/all_gather | solution.py:21
  36.2 187.6 %copy-start.2 = (f32[4096]{0:T(1024)}, f32[4096]{0:T(1024)S(1)}, u32[]{:S(2)}) copy-start(f32[4096]{0:T(1024)S(1)} %convert_element_type.78) | copy-start | bytes 49156
  36.2 184.0 %copy-start.6 = (f32[4,256]{1,0:T(4,128)S(1)}, f32[4,256]{1,0:T(4,128)}, u32[]{:S(2)}) copy-start(f32[4,256]{1,0:T(4,128)} %param.21) | copy-start | bytes 12292
  217.1 3.8 collective-permute-start
  223.7 8.9 %copy-start.8 = (f32[8]{0:T(128)S(1)}, f32[8]{0:T(128)}, u32[]{:S(2)}) copy-start(f32[8]{0:T(128)} %param.23) | copy-start | bytes 100
  223.7 8.9 %copy-start.9 = (f32[8]{0:T(128)S(1)}, f32[8]{0:T(128)}, u32[]{:S(2)}) copy-start(f32[8]{0:T(128)} %param.22) | copy-start | bytes 100
  228.5 6.9 %copy-start = (f32[4,128,8,64]{1,3,2,0:T(8,128)S(1)}, f32[4,128,8,64]{1,3,2,0:T(8,128)}, u32[]{:S(2)}) copy-start(f32[4,128,8,64]{1,3,2,0:T(8,128)} %copy.51) | copy-start | bytes 3145732
  228.6 5.1 collective-permute-start.1
  234.5 0.7 copy-start.1
  280.4 224.7 %copy-start.10 = (f32[8]{0:T(128)S(1)}, f32[8]{0:T(128)}, u32[]{:S(2)}) copy-start(f32[8]{0:T(128)} %param.24) | copy-start | bytes 100
  281.2 299.5 %all-gather.8.cloned.1.call-start = ((), (), s32[]{:S(2)}) async-start(), calls=%async_computation.2 | async-start | bytes 4259840 | tf_op jit(solution)/shard_map/all_gather | solution.py:106
  437.6 143.1 %copy-start.3 = (f32[4096]{0:T(1024)S(1)}, f32[4096]{0:T(1024)}, u32[]{:S(2)}) copy-start(f32[4096]{0:T(1024)} %copy-done.2) | copy-start | bytes 49156
  507.0 101.3 %copy-start.7 = (f32[512]{0:T(512)S(1)}, f32[512]{0:T(512)}, u32[]{:S(2)}) copy-start(f32[512]{0:T(512)} %param.25) | copy-start | bytes 6148
Sparse Core Ops, SparseCore 0:
  39.1 172.1 all-gather.5
  281.3 156.2 all-gather.9
  440.5 140.1 all-gather.7
